TPU v7x, 32 devices: a whole 2x2x4 slice. The times are simulated.
32 devices in a mesh: dp: 4 (over y, x), seq: 8 (over z, core).
Axes of the slice: x: 2, y: 2, z: 4, core: 2. Of those that a mesh axis runs over, the one named last changes fastest.
Arguments:
- features: bfloat16 [32, 16, 32, 512], P('dp', 'seq'), may hold values from -6 to 6
- conv_weight: bfloat16 [3, 3, 3, 16, 512], replicated, may hold values from -0.0546875 to 0.0546875
- clip_frames: int32 [8], replicated, may hold values from 1 to 7, as said below
- clip_group: int32 [8], replicated, may hold values from 0 to 3, as said below
- clip_offset: int32 [8], replicated, may hold values from 0 to 7, as said below
- clip_times: float32 [8], replicated, may hold values from 0.05 to 0.95
- noise_tokens: bfloat16 [4, 1024, 64], P('dp', 'seq'), may hold values from -6 to 6
- embed_weight: bfloat16 [64, 2048], replicated, may hold values from -0.75 to 0.75
- attention_proj: bfloat16 [2048, 3, 8, 128], P(None, None, 'seq'), may hold values from -0.125 to 0.125
- norm_gains: float32 [2, 128], replicated, may hold values from 0.5 to 1.5
- cotangent: bfloat16 [4, 1024, 1024], P('dp', 'seq'), may hold values from -0.09375 to 0.09375
Outputs:
- noisy_tokens: float32 [4, 1024, 64], P('dp', 'seq')
- attention_out: bfloat16 [4, 1024, 1024], P('dp', 'seq')
- proj_grad: float32 [2048, 3, 8, 128], P('dp', None, 'seq')
- norm_grad: float32 [2, 128], replicated
Inputs may be any that keep to these rules, and one draw needn't show every extreme that they name: `clip_frames`: clips follow one another along time from frame 0 and together cover all 32 frames. `clip_group`: every group trains on exactly two clips, whose frames add up to 8. `clip_offset`: the clips of one group take consecutive frame slots from slot 0 in their time order and fill all 8 slots of the group.
All inputs are finite; a program needn't handle non-finite values.
Results may differ from a plain program's by a relative error of at most 0.014.
Values may be sent and summed in bfloat16 or wider, within the bound.
No kernel may reach another device: no remote copies, remote signals or barrier semaphores. Data moves between devices by JAX's collectives and lax.ppermute only.
A program may use at most 128 MiB of HBM per device.

v0:
```python
import jax
import jax.numpy as jnp
from jax import lax
from jax.sharding import PartitionSpec as P


def shifted(block, axis, distance):
    devices = range(lax.axis_size(axis))
    route = [(i - distance, i) for i in devices if i - distance in devices]
    return lax.ppermute(block, axis, route)


def padded_2(array, sides, width):
    for axis, dim in sides:
        peers, length = (lax.axis_size(axis), array.shape[dim])
        up = [(i, (i + 1) % peers) for i in range(peers - 1)]
        down = [(j, i) for i, j in up]
        last = lax.slice_in_dim(array, length - width, length, axis=dim)
        first = lax.slice_in_dim(array, 0, width, axis=dim)
        before = lax.ppermute(last, axis, up)
        after = lax.ppermute(first, axis, down)
        array = jnp.concatenate([before, array, after], axis=dim)
    return array


def clip_bounds(clip_frames):
    ends_at = jnp.cumsum(clip_frames)
    return (ends_at - clip_frames, ends_at)


def frame_start(frame_ids, starts_at, ends_at):
    member = (frame_ids[:, None] >= starts_at[None, :]) & (frame_ids[:, None] < ends_at[None, :])
    own_start = jnp.sum(jnp.where(member, starts_at[None, :], 0), axis=1)
    return (own_start, member)


def slot_table(group_id, slot_ids, clip_group, clip_offset, clip_frames, starts_at, clip_times):
    member = (
        (clip_group[None, :] == group_id)
        & (slot_ids[:, None] >= clip_offset[None, :])
        & (slot_ids[:, None] < clip_offset[None, :] + clip_frames[None, :])
    )
    numbers = jnp.arange(clip_frames.shape[0])
    usable = jnp.any(member, axis=1).astype(jnp.float32)
    segment = jnp.sum(jnp.where(member, numbers[None, :] + 1, 0), axis=1) - 1
    source = jnp.sum(
        jnp.where(member, starts_at[None, :] + slot_ids[:, None] - clip_offset[None, :], 0), axis=1
    )
    noise_level = jnp.sum(
        jnp.where(member, clip_times[None, :], jnp.zeros((), clip_times.dtype)), axis=1
    )
    return (usable, segment, source, noise_level)


def rms_scale(values, gain_row):
    inverse = lax.rsqrt(jnp.mean(values * values, axis=-1, keepdims=True) + 1e-06)
    return (values * inverse * gain_row, inverse)


def rms_back(values, inverse, gain_row, upstream):
    scaled = gain_row * upstream
    grad_in = inverse * scaled - values * inverse**3 * jnp.mean(
        values * scaled, axis=-1, keepdims=True
    )
    gain_part = jnp.sum(upstream * values * inverse, axis=(0, 1))
    return (grad_in, gain_part)


def body(
    features,
    conv_weight,
    clip_frames,
    clip_group,
    clip_offset,
    clip_times,
    noise_tokens,
    embed_weight,
    attention_proj,
    norm_gains,
    cotangent,
):
    slab_id = lax.axis_index("dp")
    groups_n = lax.axis_size("dp")
    seq_n = lax.axis_size("seq")
    frames_dev = features.shape[0]
    width_n = features.shape[2]
    channels = features.shape[3]
    tokens_row = width_n // 2
    tok_dev = noise_tokens.shape[1]
    patch_ch = noise_tokens.shape[2]
    latent_ch = conv_weight.shape[3]
    starts_at, ends_at = clip_bounds(clip_frames)
    local_ids = jnp.arange(frames_dev)
    frame_ids = slab_id * frames_dev + local_ids
    own_start, member = frame_start(frame_ids, starts_at, ends_at)
    activated = jax.nn.silu(features.astype(jnp.float32)).astype(jnp.bfloat16)
    before = shifted(activated[frames_dev - 2 :], "dp", 1)
    extended = jnp.concatenate([before, activated], axis=0)
    rimmed = padded_2(extended, (("seq", 1),), 1)
    padded = jnp.pad(rimmed, ((0, 0), (0, 0), (1, 1), (0, 0)))
    voxels = frames_dev * 2 * width_n
    latent = jnp.zeros((latent_ch, voxels), jnp.float32)
    for tap_time in range(3):
        allowed = (frame_ids - (2 - tap_time) >= own_start).astype(jnp.float32)
        allowed_cols = jnp.repeat(allowed, 2 * width_n)[None, :]
        for tap_row in range(3):
            for tap_col in range(3):
                tap_piece = padded[
                    tap_time : tap_time + frames_dev,
                    tap_row : tap_row + 2,
                    tap_col : tap_col + width_n,
                ].reshape(voxels, channels)
                tap_term = lax.dot_general(
                    conv_weight[tap_time, tap_row, tap_col],
                    tap_piece,
                    (((1,), (1,)), ((), ())),
                    preferred_element_type=jnp.float32,
                )
                latent = latent + allowed_cols * tap_term
    patches = (
        latent.reshape(latent_ch, frames_dev, 2, tokens_row, 2)
        .transpose(1, 3, 2, 4, 0)
        .reshape(frames_dev, tokens_row, patch_ch)
    )
    usable, segment, source, noise_level = slot_table(
        slab_id, local_ids, clip_group, clip_offset, clip_frames, starts_at, clip_times
    )
    target = jnp.sum(
        jnp.where(
            member,
            clip_group[None, :] * frames_dev
            + clip_offset[None, :]
            + frame_ids[:, None]
            - starts_at[None, :],
            0,
        ),
        axis=1,
    )
    inclip = jnp.any(member, axis=1)
    slot_all = jnp.arange(groups_n * frames_dev)
    placement = ((target[:, None] == slot_all[None, :]) & inclip[:, None]).astype(jnp.float32)
    placed = jnp.einsum("fs,fcj->scj", placement, patches, precision=lax.Precision.HIGHEST).reshape(
        groups_n, frames_dev, tokens_row, patch_ch
    )
    arrived = lax.psum_scatter(placed, "dp", scatter_dimension=0, tiled=True)[0]
    noise_slots = noise_tokens.reshape(frames_dev, tokens_row, patch_ch).astype(jnp.float32)
    noisy_slots = usable[:, None, None] * (
        (1.0 - noise_level[:, None, None]) * arrived + noise_level[:, None, None] * noise_slots
    )
    noisy_out = noisy_slots.reshape(1, tok_dev, patch_ch)
    token_bf = noisy_slots.reshape(tok_dev, patch_ch).astype(jnp.bfloat16)
    all_tokens = lax.all_gather(token_bf, "seq", axis=0, tiled=True)
    hidden = jnp.dot(all_tokens, embed_weight, preferred_element_type=jnp.float32).astype(
        jnp.bfloat16
    )
    seq_len = hidden.shape[0]
    model_n = attention_proj.shape[0]
    heads_dev = attention_proj.shape[2]
    head_dim = attention_proj.shape[3]
    mixed_all = jnp.dot(
        hidden,
        attention_proj.reshape(model_n, 3 * heads_dev * head_dim),
        preferred_element_type=jnp.float32,
    ).reshape(seq_len, 3, heads_dev, head_dim)
    query_n, query_inv = rms_scale(mixed_all[:, 0], norm_gains[0])
    key_n, key_inv = rms_scale(mixed_all[:, 1], norm_gains[1])
    query_bf = query_n.astype(jnp.bfloat16)
    key_bf = key_n.astype(jnp.bfloat16)
    value_bf = mixed_all[:, 2].astype(jnp.bfloat16)
    cot_rows = cotangent.reshape(tok_dev, seq_n * heads_dev, head_dim)
    incoming = lax.all_to_all(cot_rows, "seq", split_axis=1, concat_axis=0, tiled=True)
    token_usable = jnp.tile(jnp.repeat(usable, tokens_row), seq_n)
    token_seg = jnp.tile(jnp.repeat(segment, tokens_row), seq_n)
    incoming = jnp.where(token_usable[:, None, None] > 0, incoming, jnp.zeros((), jnp.bfloat16))
    score_scale = head_dim ** (-0.5)
    block_n = min(512, seq_len)
    block_count = seq_len // block_n

    def block_step(running, inputs):
        key_grad, value_grad = running
        query_blk, grad_blk, seg_blk, keep_blk = inputs
        scores = (
            jnp.einsum("bhe,she->hbs", query_blk, key_bf, preferred_element_type=jnp.float32)
            * score_scale
        )
        same_clip = seg_blk[:, None] == token_seg[None, :]
        exp_scores = jnp.where(same_clip[None], jnp.exp(scores), 0.0)
        prob_rows = exp_scores / jnp.sum(exp_scores, axis=2, keepdims=True)
        probs_bf = prob_rows.astype(jnp.bfloat16)
        output = jnp.einsum("hbs,she->bhe", probs_bf, value_bf, preferred_element_type=jnp.float32)
        prob_grad = jnp.einsum(
            "bhe,she->hbs", grad_blk, value_bf, preferred_element_type=jnp.float32
        )
        row_delta = jnp.sum(prob_rows * prob_grad, axis=2, keepdims=True)
        score_grad = (prob_rows * (prob_grad - row_delta) * score_scale).astype(jnp.bfloat16)
        query_grad = jnp.einsum(
            "hbs,she->bhe", score_grad, key_bf, preferred_element_type=jnp.float32
        )
        key_grad = key_grad + jnp.einsum(
            "hbs,bhe->she", score_grad, query_blk, preferred_element_type=jnp.float32
        )
        value_grad = value_grad + jnp.einsum(
            "hbs,bhe->she", probs_bf, grad_blk, preferred_element_type=jnp.float32
        )
        shown_rows = (keep_blk[:, None, None] * output).astype(jnp.bfloat16)
        return ((key_grad, value_grad), (shown_rows, query_grad))

    start_state = (
        jnp.zeros((seq_len, heads_dev, head_dim), jnp.float32),
        jnp.zeros((seq_len, heads_dev, head_dim), jnp.float32),
    )
    scan_inputs = (
        query_bf.reshape(block_count, block_n, heads_dev, head_dim),
        incoming.reshape(block_count, block_n, heads_dev, head_dim),
        token_seg.reshape(block_count, block_n),
        token_usable.reshape(block_count, block_n),
    )
    final_state, scan_out = lax.scan(block_step, start_state, scan_inputs)
    key_grad, value_grad = final_state
    shown_rows = scan_out[0].reshape(seq_len, heads_dev, head_dim)
    query_grad = scan_out[1].reshape(seq_len, heads_dev, head_dim)
    token_out = lax.all_to_all(shown_rows, "seq", split_axis=0, concat_axis=1, tiled=True).reshape(
        1, tok_dev, seq_n * heads_dev * head_dim
    )
    query_in, query_gain = rms_back(mixed_all[:, 0], query_inv, norm_gains[0], query_grad)
    key_in, key_gain = rms_back(mixed_all[:, 1], key_inv, norm_gains[1], key_grad)
    stacked = (
        jnp.stack([query_in, key_in, value_grad], axis=1)
        .astype(jnp.bfloat16)
        .reshape(seq_len, 3 * heads_dev * head_dim)
    )
    proj_term = lax.dot_general(
        hidden, stacked, (((0,), (0,)), ((), ())), preferred_element_type=jnp.float32
    ).reshape(model_n, 3, heads_dev, head_dim)
    proj_grad = lax.psum_scatter(
        proj_term.astype(jnp.bfloat16), "dp", scatter_dimension=0, tiled=True
    ).astype(jnp.float32)
    norm_grad = lax.psum(jnp.stack([query_gain, key_gain]), ("dp", "seq"))
    return (noisy_out, token_out, proj_grad, norm_grad)


def solution(mesh):
    return jax.shard_map(
        body,
        mesh=mesh,
        in_specs=(
            P("dp", "seq", None, None),
            P(),
            P(),
            P(),
            P(),
            P(),
            P("dp", "seq", None),
            P(),
            P(None, None, "seq", None),
            P(),
            P("dp", "seq", None),
        ),
        out_specs=(P("dp", "seq", None), P("dp", "seq", None), P("dp", None, "seq", None), P()),
        check_vma=False,
    )
```

profile of v0, /device:TPU:0, one launch (start us, length us, event | category | flops | bytes accessed | tf_op | source)
XLA Modules:
  0.0 184.2 jit_solution(17510102135642764268)
XLA Ops:
  7.2 1.4 fusion.79
  8.7 5.0 %collective-permute-start = (bf16[2,2,32,512]{3,2,1,0:T(8,128)(2,1)S(1)}, bf16[2,2,32,512]{3,2,1,0:T(8,128)(2,1)S(1)}, u32[]{:S(2)}, u32[]{:S(2)}) collective-permute-start(bf16[2,2,32,512]{3,2,1,0:T(8,128)(2,1)S(1)} %slice.274), channel_id=1, source_target_pairs={{0,8},{8,16},{16,24},{1,9},{9,17},{17,25},{2,10},{10,18},{18,26},{... | collective-permute-start | bytes 393224 | tf_op jit(solution)/shard_map/ppermute | solution.py:10
  13.7 1.8 copy.118
  15.5 4.9 %all-to-all-start = ((bf16[128,8,128]{0,2,1:T(8,128)(2,1)}), bf16[128,8,128]{0,2,1:T(8,128)(2,1)}, u32[]{:S(2)}, u32[]{:S(2)}) async-start(bf16[128,8,128]{0,2,1:T(8,128)(2,1)} %bitcast.89), calls=%async_computation | async-start | bytes 524288 | tf_op jit(solution)/shard_map/all_to_all | solution.py:171
  22.7 2.4 %collective-permute-start.1 = (bf16[10,1,32,512]{3,2,1,0:T(8,128)(2,1)S(1)}, bf16[10,1,32,512]{3,2,1,0:T(8,128)(2,1)S(1)}, u32[]{:S(2)}, u32[]{:S(2)}) collective-permute-start(bf16[10,1,32,512]{3,2,1,0:T(8,128)(2,1)S(1)} %get-tuple-element.273), channel_id=1, source_target_pairs={{0,1},{1,2},{2,3},{3,4},{4,5},{5,6},{6,7},{8,9},{9,10},{10,11},{11... | collective-permute-start | bytes 983048 | tf_op jit(solution)/shard_map/ppermute | solution.py:20
  25.1 1.3 collective-permute-start.2
  26.7 3.0 %collective-permute-done.2 = bf16[10,1,32,512]{3,2,1,0:T(8,128)(2,1)S(1)} collective-permute-done((bf16[10,1,32,512]{3,2,1,0:T(8,128)(2,1)S(1)}, bf16[10,1,32,512]{3,2,1,0:T(8,128)(2,1)S(1)}, u32[]{:S(2)}, u32[]{:S(2)}) %collective-permute-start.2) | collective-permute-done | bytes 327712 | tf_op jit(solution)/shard_map/ppermute | solution.py:21
  30.8 0.9 select_maximum_fusion
  31.7 3.3 %fusion.174 = (bf16[8,2,32,512]{3,2,1,0:T(8,128)(2,1)S(1)}, bf16[8,2,32,512]{3,2,1,0:T(8,128)(2,1)S(1)}, bf16[8,2,32,512]{3,2,1,0:T(8,128)(2,1)S(1)}, bf16[8,2,3...) fusion(bf16[10,4,34,512]{3,2,1,0:T(8,128)(2,1)S(1)} %select_max, ...), kind=kLoop, calls=%fused_computation.266 | loop fusion | bytes 18874368 | tf_op jit(solution)/shard_map/slice | solution.py:108
  41.5 1.0 fusion.161
  42.6 0.7 broadcast_bitcast_fusion.1
  43.8 0.7 copy.115
  44.5 1.1 copy.119
  45.7 0.9 fusion.93
  46.5 24.6 %reduce-scatter.7.cloned.1.call-done = f32[1,8,16,64]{3,1,2,0:T(8,128)} async-done(((f32[4,8,16,64]{3,1,2,0:T(8,128)}), f32[1,8,16,64]{3,1,2,0:T(8,128)}) %reduce-scatter.7.cloned.1.call-update) | async-done | bytes 32784
  71.1 0.9 copy.112
  72.2 14.5 %all_gather.3 = bf16[1024,64]{1,0:T(8,128)(2,1)S(1)} all-gather(bf16[128,64]{1,0:T(8,128)(2,1)S(1)} %fusion.99), channel_id=1, replica_groups=mesh['dp'=4,'seq'=8] {'seq'}, dimensions={0}, use_global_device_ids=true | all-gather | bytes 147456 | tf_op jit(solution)/shard_map/all_gather | solution.py:152
  86.7 1.2 convolution_convert_fusion
  87.9 1.8 fusion.30
  90.1 1.0 copy-done.3
  91.6 0.8 copy.123
  92.6 23.3 %while.17 = (s32[]{:T(128)}, f32[1024,1,128]{0,2,1:T(8,128)}, f32[1024,1,128]{0,2,1:T(8,128)}, bf16[2,512,1,128]{3,1,2,0:T(8,128)(2,1)}, f32[2,512,1,128]{3,1,2,...) while((s32[]{:T(128)}, f32[1024,1,128]{0,2,1:T(8,128)}, ...), condition=%wide.region_13.14_spmd.clone, body=%wide.region_10.13_spmd.clone.sunk | while | flops 814349312 | bytes 36606396 | solution.py:218
  93.4 1.5 multiply_reduce_fusion.5
  95.4 2.1 %fusion.232 = f32[1024,1,128]{0,2,1:T(8,128)} fusion(bf16[512,1024]{1,0:T(8,128)(2,1)S(1)} %multiply_convert_fusion.4, f32[1024,1,128]{0,2,1:T(8,128)} %get-tuple-element.389, pred[]{:T(512)S(6)} %compare.42, bf16[2,512,1,128]{3,1,2,0:T(8,128)(2,1)} %copy-done.7, s32[]{:T(128)} %get-tuple-element.388), kind=kOutput, calls=%fused_computation.6.clone.1 | convolution fusion | flops 134479872 | bytes 2228737 | tf_op jit(solution)/shard_map/while/body/eval_jaxpr/hbs,bhe->she/dot_general | solution.py:199
  97.5 1.4 fusion.235
  98.9 0.8 copy-done.10
  99.7 1.4 fusion.233
  101.1 0.8 copy-done.17
  101.9 1.6 fusion.234
  103.5 0.7 copy-done.14
  104.9 1.6 multiply_reduce_fusion.5
  106.9 2.3 %fusion.232 = f32[1024,1,128]{0,2,1:T(8,128)} fusion(bf16[512,1024]{1,0:T(8,128)(2,1)S(1)} %multiply_convert_fusion.4, f32[1024,1,128]{0,2,1:T(8,128)} %get-tuple-element.389, pred[]{:T(512)S(6)} %compare.42, bf16[2,512,1,128]{3,1,2,0:T(8,128)(2,1)} %copy-done.7, s32[]{:T(128)} %get-tuple-element.388), kind=kOutput, calls=%fused_computation.6.clone.1 | convolution fusion | flops 134479872 | bytes 2228737 | tf_op jit(solution)/shard_map/while/body/eval_jaxpr/hbs,bhe->she/dot_general | solution.py:199
  109.3 1.4 fusion.235
  110.6 0.8 copy-done.10
  111.4 1.4 fusion.233
  112.9 0.8 copy-done.17
  113.6 1.6 fusion.234
  115.2 0.7 copy-done.14
  115.9 1.4 copy.138
  117.3 1.2 fusion.88
  118.9 1.1 convert_bitcast_fusion
  120.3 5.8 %fusion.36 = bf16[2048,3,1,128]{3,0,1,2:T(8,128)(2,1)} fusion(bf16[1024,2048]{1,0:T(8,128)(2,1)} %copy-done.2, bf16[1024,1,1,128]{0,3,2,1:T(8,128)(2,1)S(1)} %convert_bitcast_fusion, bf16[1024,1,1,128]{0,3,2,1:T(8,128)(2,1)S(1)} %fusion.91, bf16[1024,1,1,128]{0,3,2,1:T(8,128)(2,1)S(1)} %subtract_convert_fusion.1), kind=kOutput, calls=%fused_computation.47 | convolution fusion | flops 1613758464 | bytes 6553600 | tf_op jit(solution)/shard_map/dot_general | solution.py:232
  126.7 0.8 reduce.8
  127.5 0.8 reshape.832
  128.2 4.5 %all-to-all-start.1 = ((bf16[8,2,8192]{2,1,0:T(2,128)(2,1)}), bf16[8,2,8192]{2,1,0:T(2,128)(2,1)S(1)}, u32[]{:S(2)}, u32[]{:S(2)}) async-start(bf16[8,2,8192]{2,1,0:T(2,128)(2,1)} %reshape.832), calls=%async_computation.1 | async-start | bytes 524288 | tf_op jit(solution)/shard_map/all_to_all | solution.py:222
  133.6 39.9 %psum.7 = f32[2,128]{1,0:T(2,128)} all-reduce(f32[2,128]{1,0:T(2,128)S(1)} %pad_maximum_fusion.2), channel_id=1, replica_groups=mesh['dp'=4,'seq'=8] {'dp','seq'}, use_global_device_ids=true, to_apply=%region_19.20 | all-reduce | flops 256 | bytes 2048 | tf_op jit(solution)/shard_map/psum | solution.py:238
  174.0 0.9 copy.130
  174.9 2.5 %copy.131 = f32[512,3,1,128]{3,2,1,0:T(1,128)} copy(bf16[512,3,1,128]{3,0,1,2:T(8,128)(2,1)} %reduce-scatter.5.cloned.1.call-done) | data formatting | bytes 1179648
  (189 shorter events, 16.5 us)
Async XLA Ops:
  7.2 79.5 %copy-start = (bf16[64,2048]{1,0:T(8,128)(2,1)S(1)}, bf16[64,2048]{1,0:T(8,128)(2,1)}, u32[]{:S(2)}) copy-start(bf16[64,2048]{1,0:T(8,128)(2,1)} %param.20) | copy-start | bytes 786436
  7.2 13.3 %copy-start.28 = (s32[8]{0:T(128)S(1)}, s32[8]{0:T(128)}, u32[]{:S(2)}) copy-start(s32[8]{0:T(128)} %param.16) | copy-start | bytes 100
  7.2 13.3 %copy-start.27 = (s32[8]{0:T(128)S(1)}, s32[8]{0:T(128)}, u32[]{:S(2)}) copy-start(s32[8]{0:T(128)} %param.15) | copy-start | bytes 100
  7.2 13.5 %copy-start.21 = (s32[8]{0:T(128)S(1)}, s32[8]{0:T(128)}, u32[]{:S(2)}) copy-start(s32[8]{0:T(128)} %param.17) | copy-start | bytes 100
  7.2 14.0 %copy-start.29 = (f32[8]{0:T(128)S(1)}, f32[8]{0:T(128)}, u32[]{:S(2)}) copy-start(f32[8]{0:T(128)} %param.18) | copy-start | bytes 100
  7.2 14.2 %copy-start.26 = (f32[2,128]{1,0:T(2,128)S(1)}, f32[2,128]{1,0:T(2,128)}, u32[]{:S(2)}) copy-start(f32[2,128]{1,0:T(2,128)} %param.22) | copy-start | bytes 3076
  8.7 17.8 %copy-start.18 = (bf16[3,3,3,16,512]{4,3,2,1,0:T(8,128)(2,1)S(1)}, bf16[3,3,3,16,512]{4,3,2,1,0:T(8,128)(2,1)}, u32[]{:S(2)}) copy-start(bf16[3,3,3,16,512]{4,3,2,1,0:T(8,128)(2,1)} %param.14) | copy-start | bytes 1327108
  8.7 13.9 %collective-permute-start = (bf16[2,2,32,512]{3,2,1,0:T(8,128)(2,1)S(1)}, bf16[2,2,32,512]{3,2,1,0:T(8,128)(2,1)S(1)}, u32[]{:S(2)}, u32[]{:S(2)}) collective-permute-start(bf16[2,2,32,512]{3,2,1,0:T(8,128)(2,1)S(1)} %slice.274), channel_id=1, source_target_pairs={{0,8},{8,16},{16,24},{1,9},{9,17},{17,25},{2,10},{10,18},{18,26},{... | collective-permute-start | bytes 393224 | tf_op jit(solution)/shard_map/ppermute | solution.py:10
  15.5 29.0 %all-to-all-start = ((bf16[128,8,128]{0,2,1:T(8,128)(2,1)}), bf16[128,8,128]{0,2,1:T(8,128)(2,1)}, u32[]{:S(2)}, u32[]{:S(2)}) async-start(bf16[128,8,128]{0,2,1:T(8,128)(2,1)} %bitcast.89), calls=%async_computation | async-start | bytes 524288 | tf_op jit(solution)/shard_map/all_to_all | solution.py:171
  20.4 50.8 %reduce-scatter.7.cloned.1.call-start = ((), (), s32[]{:S(2)}) async-start(), calls=%async_computation.5 | async-start | bytes 327680
  22.7 4.0 %collective-permute-start.1 = (bf16[10,1,32,512]{3,2,1,0:T(8,128)(2,1)S(1)}, bf16[10,1,32,512]{3,2,1,0:T(8,128)(2,1)S(1)}, u32[]{:S(2)}, u32[]{:S(2)}) collective-permute-start(bf16[10,1,32,512]{3,2,1,0:T(8,128)(2,1)S(1)} %get-tuple-element.273), channel_id=1, source_target_pairs={{0,1},{1,2},{2,3},{3,4},{4,5},{5,6},{6,7},{8,9},{9,10},{10,11},{11... | collective-permute-start | bytes 983048 | tf_op jit(solution)/shard_map/ppermute | solution.py:20
  25.1 4.6 %collective-permute-start.2 = (bf16[10,1,32,512]{3,2,1,0:T(8,128)(2,1)S(1)}, bf16[10,1,32,512]{3,2,1,0:T(8,128)(2,1)S(1)}, u32[]{:S(2)}, u32[]{:S(2)}) collective-permute-start(bf16[10,1,32,512]{3,2,1,0:T(8,128)(2,1)S(1)} %get-tuple-element.274), channel_id=1, source_target_pairs={{1,0},{2,1},{3,2},{4,3},{5,4},{6,5},{7,6},{9,8},{10,9},{11,10},{12... | collective-permute-start | bytes 983048 | tf_op jit(solution)/shard_map/ppermute | solution.py:21
  40.0 3.7 %copy-start.19 = (bf16[1,128,64]{1,2,0:T(8,128)(2,1)S(1)}, bf16[1,128,64]{1,2,0:T(8,128)(2,1)}, u32[]{:S(2)}) copy-start(bf16[1,128,64]{1,2,0:T(8,128)(2,1)} %param.19) | copy-start | bytes 49156
  40.3 3.5 %copy-start.12 = (bf16[2048,3,1,128]{3,0,2,1:T(8,128)(2,1)S(1)}, bf16[2048,3,1,128]{3,0,2,1:T(8,128)(2,1)}, u32[]{:S(2)}) copy-start(bf16[2048,3,1,128]{3,0,2,1:T(8,128)(2,1)} %param.21) | copy-start | bytes 4718596
  42.6 132.3 %reduce-scatter.5.cloned.1.call-start = ((), (), s32[]{:S(2)}) async-start(), calls=%async_computation.4 | async-start | bytes 1966080 | tf_op jit(solution)/shard_map/reduce_scatter | solution.py:235
  43.5 28.5 %copy-start.22 = (f32[128]{0:T(128)}, f32[128]{0:T(128)S(1)}, u32[]{:S(2)}) copy-start(f32[128]{0:T(128)S(1)} %mul.598) | copy-start | bytes 1540
  43.7 28.3 %copy-start.24 = (f32[128]{0:T(128)}, f32[128]{0:T(128)S(1)}, u32[]{:S(2)}) copy-start(f32[128]{0:T(128)S(1)} %mul.661) | copy-start | bytes 1540
  87.9 1.9 %copy-start.2 = (bf16[1024,2048]{1,0:T(8,128)(2,1)}, bf16[1024,2048]{1,0:T(8,128)(2,1)S(1)}, u32[]{:S(2)}) copy-start(bf16[1024,2048]{1,0:T(8,128)(2,1)S(1)} %convolution_convert_fusion) | copy-start | bytes 12582916
  89.9 1.2 copy-start.3
  90.0 2.6 %copy-start.20 = (s32[512]{0:T(512)S(1)}, s32[512]{0:T(512)}, u32[]{:S(2)}) copy-start(s32[512]{0:T(512)} %broadcast_bitcast_fusion.3) | copy-start | bytes 6148
  92.6 2.3 %copy-start.5 = (bf16[1024,1,128]{2,0,1:T(8,128)(2,1)}, bf16[1024,1,128]{2,0,1:T(8,128)(2,1)S(1)}, u32[]{:S(2)}) copy-start(bf16[1024,1,128]{2,0,1:T(8,128)(2,1)S(1)} %get-tuple-element.409) | copy-start | bytes 786436 | tf_op jit(solution)/shard_map/while
  92.7 2.3 %copy-start.7 = (bf16[2,512,1,128]{3,1,2,0:T(8,128)(2,1)}, bf16[2,512,1,128]{3,1,2,0:T(8,128)(2,1)S(1)}, u32[]{:S(2)}) copy-start(bf16[2,512,1,128]{3,1,2,0:T(8,128)(2,1)S(1)} %get-tuple-element.407) | copy-start | bytes 786436 | tf_op jit(solution)/shard_map/while
  95.4 2.1 %copy-start.9 = (f32[2,512,1,128]{3,1,2,0:T(8,128)S(1)}, f32[2,512,1,128]{3,1,2,0:T(8,128)}, u32[]{:S(2)}) copy-start(f32[2,512,1,128]{3,1,2,0:T(8,128)} %get-tuple-element.392) | copy-start | bytes 1572868 | tf_op jit(solution)/shard_map/while
  95.4 4.3 %copy-start.16 = (f32[1024,1,128]{0,2,1:T(8,128)S(1)}, f32[1024,1,128]{0,2,1:T(8,128)}, u32[]{:S(2)}) copy-start(f32[1024,1,128]{0,2,1:T(8,128)} %get-tuple-element.390) | copy-start | bytes 1572868 | tf_op jit(solution)/shard_map/while
  98.9 0.8 copy-start.10
  99.7 2.2 %copy-start.13 = (bf16[2,512,1,128]{3,1,2,0:T(8,128)(2,1)S(1)}, bf16[2,512,1,128]{3,1,2,0:T(8,128)(2,1)}, u32[]{:S(2)}) copy-start(bf16[2,512,1,128]{3,1,2,0:T(8,128)(2,1)} %get-tuple-element.391) | copy-start | bytes 786436 | tf_op jit(solution)/shard_map/while
  101.1 0.8 copy-start.17
  101.9 2.3 %copy-start.6 = (bf16[1024,1,128]{2,0,1:T(8,128)(2,1)S(1)}, bf16[1024,1,128]{2,0,1:T(8,128)(2,1)}, u32[]{:S(2)}) copy-start(bf16[1024,1,128]{2,0,1:T(8,128)(2,1)} %copy-done.5) | copy-start | bytes 786436 | tf_op jit(solution)/shard_map/while
  101.9 2.3 %copy-start.8 = (bf16[2,512,1,128]{3,1,2,0:T(8,128)(2,1)S(1)}, bf16[2,512,1,128]{3,1,2,0:T(8,128)(2,1)}, u32[]{:S(2)}) copy-start(bf16[2,512,1,128]{3,1,2,0:T(8,128)(2,1)} %copy-done.7) | copy-start | bytes 786436 | tf_op jit(solution)/shard_map/while
  103.5 0.7 copy-start.14
  104.2 2.3 %copy-start.5 = (bf16[1024,1,128]{2,0,1:T(8,128)(2,1)}, bf16[1024,1,128]{2,0,1:T(8,128)(2,1)S(1)}, u32[]{:S(2)}) copy-start(bf16[1024,1,128]{2,0,1:T(8,128)(2,1)S(1)} %get-tuple-element.409) | copy-start | bytes 786436 | tf_op jit(solution)/shard_map/while
  104.2 2.3 %copy-start.7 = (bf16[2,512,1,128]{3,1,2,0:T(8,128)(2,1)}, bf16[2,512,1,128]{3,1,2,0:T(8,128)(2,1)S(1)}, u32[]{:S(2)}) copy-start(bf16[2,512,1,128]{3,1,2,0:T(8,128)(2,1)S(1)} %get-tuple-element.407) | copy-start | bytes 786436 | tf_op jit(solution)/shard_map/while
  106.9 2.3 %copy-start.9 = (f32[2,512,1,128]{3,1,2,0:T(8,128)S(1)}, f32[2,512,1,128]{3,1,2,0:T(8,128)}, u32[]{:S(2)}) copy-start(f32[2,512,1,128]{3,1,2,0:T(8,128)} %get-tuple-element.392) | copy-start | bytes 1572868 | tf_op jit(solution)/shard_map/while
  106.9 4.5 %copy-start.16 = (f32[1024,1,128]{0,2,1:T(8,128)S(1)}, f32[1024,1,128]{0,2,1:T(8,128)}, u32[]{:S(2)}) copy-start(f32[1024,1,128]{0,2,1:T(8,128)} %get-tuple-element.390) | copy-start | bytes 1572868 | tf_op jit(solution)/shard_map/while
  110.6 0.8 copy-start.10
  111.4 2.2 %copy-start.13 = (bf16[2,512,1,128]{3,1,2,0:T(8,128)(2,1)S(1)}, bf16[2,512,1,128]{3,1,2,0:T(8,128)(2,1)}, u32[]{:S(2)}) copy-start(bf16[2,512,1,128]{3,1,2,0:T(8,128)(2,1)} %get-tuple-element.391) | copy-start | bytes 786436 | tf_op jit(solution)/shard_map/while
  112.8 0.8 copy-start.17
  113.6 2.3 %copy-start.6 = (bf16[1024,1,128]{2,0,1:T(8,128)(2,1)S(1)}, bf16[1024,1,128]{2,0,1:T(8,128)(2,1)}, u32[]{:S(2)}) copy-start(bf16[1024,1,128]{2,0,1:T(8,128)(2,1)} %copy-done.5) | copy-start | bytes 786436 | tf_op jit(solution)/shard_map/while
  113.6 2.3 %copy-start.8 = (bf16[2,512,1,128]{3,1,2,0:T(8,128)(2,1)S(1)}, bf16[2,512,1,128]{3,1,2,0:T(8,128)(2,1)}, u32[]{:S(2)}) copy-start(bf16[2,512,1,128]{3,1,2,0:T(8,128)(2,1)} %copy-done.7) | copy-start | bytes 786436 | tf_op jit(solution)/shard_map/while
  115.2 0.7 copy-start.14
  115.9 2.6 %copy-start.1 = (f32[1024,1,128]{0,2,1:T(8,128)S(1)}, f32[1024,1,128]{0,2,1:T(8,128)}, u32[]{:S(2)}) copy-start(f32[1024,1,128]{0,2,1:T(8,128)} %get-tuple-element.71) | copy-start | bytes 1572868
  115.9 2.6 %copy-start.4 = (f32[1024,3,128]{0,2,1:T(8,128)S(1)}, f32[1024,3,128]{0,2,1:T(8,128)}, u32[]{:S(2)}) copy-start(f32[1024,3,128]{0,2,1:T(8,128)} %copy-done.3) | copy-start | bytes 4718596
  115.9 2.8 %copy-start.11 = (f32[2,512,1,128]{3,1,2,0:T(8,128)S(1)}, f32[2,512,1,128]{3,1,2,0:T(8,128)}, u32[]{:S(2)}) copy-start(f32[2,512,1,128]{3,1,2,0:T(8,128)} %get-tuple-element.70) | copy-start | bytes 1572868
  120.3 6.4 %copy-start.15 = (bf16[2,512,1,128]{3,1,2,0:T(8,128)(2,1)S(1)}, bf16[2,512,1,128]{3,1,2,0:T(8,128)(2,1)}, u32[]{:S(2)}) copy-start(bf16[2,512,1,128]{3,1,2,0:T(8,128)(2,1)} %get-tuple-element.69) | copy-start | bytes 786436
  126.1 6.6 %copy-start.23 = (f32[128]{0:T(128)S(1)}, f32[128]{0:T(128)}, u32[]{:S(2)}) copy-start(f32[128]{0:T(128)} %copy-done.22) | copy-start | bytes 1540
  126.1 6.6 %copy-start.25 = (f32[128]{0:T(128)S(1)}, f32[128]{0:T(128)}, u32[]{:S(2)}) copy-start(f32[128]{0:T(128)} %copy-done.24) | copy-start | bytes 1540
  128.2 45.3 %all-to-all-start.1 = ((bf16[8,2,8192]{2,1,0:T(2,128)(2,1)}), bf16[8,2,8192]{2,1,0:T(2,128)(2,1)S(1)}, u32[]{:S(2)}, u32[]{:S(2)}) async-start(bf16[8,2,8192]{2,1,0:T(2,128)(2,1)} %reshape.832), calls=%async_computation.1 | async-start | bytes 524288 | tf_op jit(solution)/shard_map/all_to_all | solution.py:222
Sparse Core Ops, SparseCore 0:
  42.7 28.4 reduce-scatter.6
  126.3 31.2 reduce-scatter.4
where the time goes:
time: 185 us; the launch traced here: 184 us
  blocking collectives  54.5 us (29%)
  matrix products  34.2 us (18%)
  waiting for transfers between devices  27.7 us (15%)
  local copies, waits for them, and re-layouts  25.5 us (14%)
  starting transfers between devices  18.1 us (10%)
  between operations  14.6 us (8%)
  other arithmetic  9.24 us (5%)
    psum x1, blocking collectives, body(): norm_grad = lax.psum(jnp.stack([query_gain, key_gain]), ('dp', 'seq'))  39.9 us
    unnamed x3, waiting for transfers between devices  24.7 us
    all_gather x1, blocking collectives, body(): all_tokens = lax.all_gather(token_bf, 'seq', axis=0, tiled=True)  14.5 us
    unnamed x52, local copies, waits for them, and re-layouts  10.6 us
    dot_general x27, matrix products, body(): lax.dot_general(conv_weight[tap_time, tap_row, tap_col], tap_piece, (((1,...  6.8 us
    dot_general x1, matrix products, body(): lax.dot_general(hidden, stacked, (((0,), (0,)), ((), ())), preferred_elem...  5.82 us
    ppermute x1, starting transfers between devices, shifted(): return lax.ppermute(block, axis, route)  5.01 us
    all_to_all x1, starting transfers between devices, body(): lax.all_to_all(cot_rows, 'seq', split_axis=1, concat_axis=0, tiled=True)  4.88 us
  transfers between devices with their start and end apart: 7, of which 2 were waited for; matrix products, arithmetic and copies ran while one was open for 14% of the time, Pallas kernels for 0%

commit v1 on v0

--- a/solution.py
+++ b/solution.py
@@ -235,7 +235,7 @@
     proj_grad = lax.psum_scatter(
         proj_term.astype(jnp.bfloat16), "dp", scatter_dimension=0, tiled=True
     ).astype(jnp.float32)
-    norm_grad = lax.psum(jnp.stack([query_gain, key_gain]), ("dp", "seq"))
+    norm_grad = lax.psum(lax.psum(jnp.stack([query_gain, key_gain]), "seq"), "dp")
     return (noisy_out, token_out, proj_grad, norm_grad)
 
 

time: 185 us -> 172 us (0.930)
  blocking collectives: 54.5 us -> 41.1 us
    psum x1 -> x2, blocking collectives: 39.9 us -> 26.6 us  [the longest x1 17.1 us: body(): lax.psum(jnp.stack([query_gain, key_gain]), 'seq')]
  transfers between devices with their start and end apart: 7 -> 7, of which waited for: 2 -> 2; matrix products, arithmetic and copies ran while one was open for 14% -> 15% of each run, Pallas kernels for 0% -> 0%
where the time goes in v1:
time: 172 us; the launch traced here: 171 us
  blocking collectives  41.1 us (24%)
  matrix products  34.2 us (20%)
  waiting for transfers between devices  27.7 us (16%)
  local copies, waits for them, and re-layouts  25.5 us (15%)
  starting transfers between devices  18.2 us (11%)
  between operations  14.6 us (8%)
  other arithmetic  9.26 us (5%)
    unnamed x3, waiting for transfers between devices  24.7 us
    psum x1, blocking collectives, body(): lax.psum(jnp.stack([query_gain, key_gain]), 'seq')  17.1 us
    all_gather x1, blocking collectives, body(): all_tokens = lax.all_gather(token_bf, 'seq', axis=0, tiled=True)  14.5 us
    unnamed x52, local copies, waits for them, and re-layouts  10.6 us
    psum x1, blocking collectives, body(): lax.psum(lax.psum(jnp.stack([query_gain, key_gain]), 'seq'), 'dp')  9.5 us
    dot_general x27, matrix products, body(): lax.dot_general(conv_weight[tap_time, tap_row, tap_col], tap_piece, (((1,...  6.8 us
    dot_general x1, matrix products, body(): lax.dot_general(hidden, stacked, (((0,), (0,)), ((), ())), preferred_elem...  5.8 us
    ppermute x1, starting transfers between devices, shifted(): return lax.ppermute(block, axis, route)  5.01 us
  transfers between devices with their start and end apart: 7, of which 2 were waited for; matrix products, arithmetic and copies ran while one was open for 15% of the time, Pallas kernels for 0%

profile of v1, /device:TPU:0, one launch (start us, length us, event | category | flops | bytes accessed | tf_op | source)
XLA Modules:
  0.0 170.9 jit_solution(6601211544273426534)
XLA Ops:
  7.2 1.4 fusion.79
  8.7 5.0 %collective-permute-start = (bf16[2,2,32,512]{3,2,1,0:T(8,128)(2,1)S(1)}, bf16[2,2,32,512]{3,2,1,0:T(8,128)(2,1)S(1)}, u32[]{:S(2)}, u32[]{:S(2)}) collective-permute-start(bf16[2,2,32,512]{3,2,1,0:T(8,128)(2,1)S(1)} %slice.274), channel_id=1, source_target_pairs={{0,8},{8,16},{16,24},{1,9},{9,17},{17,25},{2,10},{10,18},{18,26},{... | collective-permute-start | bytes 393224 | tf_op jit(solution)/shard_map/ppermute | solution.py:10
  13.7 1.8 %copy.118 = bf16[1,128,1024]{1,2,0:T(8,128)(2,1)} copy(bf16[1,128,1024]{2,1,0:T(8,128)(2,1)} %param.23) | data formatting | bytes 524288 | tf_op args[10]
  15.5 4.9 %all-to-all-start = ((bf16[128,8,128]{0,2,1:T(8,128)(2,1)}), bf16[128,8,128]{0,2,1:T(8,128)(2,1)}, u32[]{:S(2)}, u32[]{:S(2)}) async-start(bf16[128,8,128]{0,2,1:T(8,128)(2,1)} %bitcast.89), calls=%async_computation | async-start | bytes 524288 | tf_op jit(solution)/shard_map/all_to_all | solution.py:171
  22.7 2.4 %collective-permute-start.1 = (bf16[10,1,32,512]{3,2,1,0:T(8,128)(2,1)S(1)}, bf16[10,1,32,512]{3,2,1,0:T(8,128)(2,1)S(1)}, u32[]{:S(2)}, u32[]{:S(2)}) collective-permute-start(bf16[10,1,32,512]{3,2,1,0:T(8,128)(2,1)S(1)} %get-tuple-element.273), channel_id=1, source_target_pairs={{0,1},{1,2},{2,3},{3,4},{4,5},{5,6},{6,7},{8,9},{9,10},{10,11},{11... | collective-permute-start | bytes 983048 | tf_op jit(solution)/shard_map/ppermute | solution.py:20
  25.1 1.3 collective-permute-start.2
  26.7 3.0 %collective-permute-done.2 = bf16[10,1,32,512]{3,2,1,0:T(8,128)(2,1)S(1)} collective-permute-done((bf16[10,1,32,512]{3,2,1,0:T(8,128)(2,1)S(1)}, bf16[10,1,32,512]{3,2,1,0:T(8,128)(2,1)S(1)}, u32[]{:S(2)}, u32[]{:S(2)}) %collective-permute-start.2) | collective-permute-done | bytes 327712 | tf_op jit(solution)/shard_map/ppermute | solution.py:21
  30.8 0.9 select_maximum_fusion
  31.7 3.3 %fusion.174 = (bf16[8,2,32,512]{3,2,1,0:T(8,128)(2,1)S(1)}, bf16[8,2,32,512]{3,2,1,0:T(8,128)(2,1)S(1)}, bf16[8,2,32,512]{3,2,1,0:T(8,128)(2,1)S(1)}, bf16[8,2,3...) fusion(bf16[10,4,34,512]{3,2,1,0:T(8,128)(2,1)S(1)} %select_max, ...), kind=kLoop, calls=%fused_computation.266 | loop fusion | bytes 18874368 | tf_op jit(solution)/shard_map/slice | solution.py:108
  41.5 1.0 fusion.161
  42.6 0.7 broadcast_bitcast_fusion.1
  44.5 1.1 copy.119
  45.7 0.9 fusion.93
  46.5 24.6 %reduce-scatter.7.cloned.1.call-done = f32[1,8,16,64]{3,1,2,0:T(8,128)} async-done(((f32[4,8,16,64]{3,1,2,0:T(8,128)}), f32[1,8,16,64]{3,1,2,0:T(8,128)}) %reduce-scatter.7.cloned.1.call-update) | async-done | bytes 32784
  71.2 0.9 copy.112
  72.2 14.5 %all_gather.3 = bf16[1024,64]{1,0:T(8,128)(2,1)S(1)} all-gather(bf16[128,64]{1,0:T(8,128)(2,1)S(1)} %fusion.99), channel_id=1, replica_groups=mesh['dp'=4,'seq'=8] {'seq'}, dimensions={0}, use_global_device_ids=true | all-gather | bytes 147456 | tf_op jit(solution)/shard_map/all_gather | solution.py:152
  86.7 1.2 convolution_convert_fusion
  87.9 1.8 %fusion.30 = f32[1024,3,128]{0,2,1:T(8,128)S(1)} fusion(bf16[1024,2048]{1,0:T(8,128)(2,1)S(1)} %convolution_convert_fusion, bf16[2048,3,1,128]{0,3,1,2:T(8,128)(2,1)S(1)} %copy.115), kind=kOutput, calls=%fused_computation.42 | convolution fusion | flops 1610612736 | bytes 7340032 | tf_op jit(solution)/shard_map/dot_general | solution.py:160
  90.1 0.9 copy-done.3
  91.5 0.8 copy.123
  92.6 23.3 %while.17 = (s32[]{:T(128)}, f32[1024,1,128]{0,2,1:T(8,128)}, f32[1024,1,128]{0,2,1:T(8,128)}, bf16[2,512,1,128]{3,1,2,0:T(8,128)(2,1)}, f32[2,512,1,128]{3,1,2,...) while((s32[]{:T(128)}, f32[1024,1,128]{0,2,1:T(8,128)}, ...), condition=%wide.region_13.14_spmd.clone, body=%wide.region_10.13_spmd.clone.sunk | while | flops 814349312 | bytes 36606396 | solution.py:218
  93.4 1.5 multiply_reduce_fusion.5
  95.4 2.1 %fusion.232 = f32[1024,1,128]{0,2,1:T(8,128)} fusion(bf16[512,1024]{1,0:T(8,128)(2,1)S(1)} %multiply_convert_fusion.4, f32[1024,1,128]{0,2,1:T(8,128)} %get-tuple-element.389, pred[]{:T(512)S(6)} %compare.42, bf16[2,512,1,128]{3,1,2,0:T(8,128)(2,1)} %copy-done.7, s32[]{:T(128)} %get-tuple-element.388), kind=kOutput, calls=%fused_computation.6.clone.1 | convolution fusion | flops 134479872 | bytes 2228737 | tf_op jit(solution)/shard_map/while/body/eval_jaxpr/hbs,bhe->she/dot_general | solution.py:199
  97.5 1.4 fusion.235
  98.9 0.8 copy-done.10
  99.7 1.4 fusion.233
  101.1 0.8 copy-done.17
  101.9 1.6 fusion.234
  103.5 0.7 copy-done.14
  104.9 1.5 multiply_reduce_fusion.5
  106.9 2.3 %fusion.232 = f32[1024,1,128]{0,2,1:T(8,128)} fusion(bf16[512,1024]{1,0:T(8,128)(2,1)S(1)} %multiply_convert_fusion.4, f32[1024,1,128]{0,2,1:T(8,128)} %get-tuple-element.389, pred[]{:T(512)S(6)} %compare.42, bf16[2,512,1,128]{3,1,2,0:T(8,128)(2,1)} %copy-done.7, s32[]{:T(128)} %get-tuple-element.388), kind=kOutput, calls=%fused_computation.6.clone.1 | convolution fusion | flops 134479872 | bytes 2228737 | tf_op jit(solution)/shard_map/while/body/eval_jaxpr/hbs,bhe->she/dot_general | solution.py:199
  109.2 1.4 fusion.235
  110.6 0.8 copy-done.10
  111.4 1.4 fusion.233
  112.9 0.8 copy-done.17
  113.6 1.6 fusion.234
  115.2 0.7 copy-done.14
  115.9 1.4 copy.138
  117.3 1.2 fusion.88
  118.9 1.1 convert_bitcast_fusion
  120.3 5.8 %fusion.36 = bf16[2048,3,1,128]{3,0,1,2:T(8,128)(2,1)} fusion(bf16[1024,2048]{1,0:T(8,128)(2,1)} %copy-done.2, bf16[1024,1,1,128]{0,3,2,1:T(8,128)(2,1)S(1)} %convert_bitcast_fusion, bf16[1024,1,1,128]{0,3,2,1:T(8,128)(2,1)S(1)} %fusion.91, bf16[1024,1,1,128]{0,3,2,1:T(8,128)(2,1)S(1)} %subtract_convert_fusion.1), kind=kOutput, calls=%fused_computation.47 | convolution fusion | flops 1613758464 | bytes 6553600 | tf_op jit(solution)/shard_map/dot_general | solution.py:232
  126.6 0.8 reduce.8
  127.4 0.8 reshape.832
  128.2 4.5 %all-to-all-start.1 = ((bf16[8,2,8192]{2,1,0:T(2,128)(2,1)}), bf16[8,2,8192]{2,1,0:T(2,128)(2,1)S(1)}, u32[]{:S(2)}, u32[]{:S(2)}) async-start(bf16[8,2,8192]{2,1,0:T(2,128)(2,1)} %reshape.832), calls=%async_computation.1 | async-start | bytes 524288 | tf_op jit(solution)/shard_map/all_to_all | solution.py:222
  133.6 17.1 %psum.14 = f32[2,128]{1,0:T(2,128)S(1)} all-reduce(f32[2,128]{1,0:T(2,128)S(1)} %pad_maximum_fusion.2), channel_id=1, replica_groups=mesh['dp'=4,'seq'=8] {'seq'}, use_global_device_ids=true, to_apply=%region_19.20 | all-reduce | flops 256 | bytes 2048 | tf_op jit(solution)/shard_map/psum | solution.py:238
  150.7 9.5 %psum.15 = f32[2,128]{1,0:T(2,128)} all-reduce(f32[2,128]{1,0:T(2,128)S(1)} %psum.14), channel_id=1, replica_groups=mesh['dp'=4,'seq'=8] {'dp'}, use_global_device_ids=true, to_apply=%region_20.21 | all-reduce | flops 256 | bytes 2048 | tf_op jit(solution)/shard_map/psum | solution.py:238
  160.7 0.9 copy.130
  161.6 2.5 %copy.131 = f32[512,3,1,128]{3,2,1,0:T(1,128)} copy(bf16[512,3,1,128]{3,0,1,2:T(8,128)(2,1)} %reduce-scatter.5.cloned.1.call-done) | data formatting | bytes 1179648
  (190 shorter events, 17.2 us)
Async XLA Ops:
  7.2 79.5 %copy-start = (bf16[64,2048]{1,0:T(8,128)(2,1)S(1)}, bf16[64,2048]{1,0:T(8,128)(2,1)}, u32[]{:S(2)}) copy-start(bf16[64,2048]{1,0:T(8,128)(2,1)} %param.20) | copy-start | bytes 786436
  7.2 13.3 %copy-start.28 = (s32[8]{0:T(128)S(1)}, s32[8]{0:T(128)}, u32[]{:S(2)}) copy-start(s32[8]{0:T(128)} %param.16) | copy-start | bytes 100
  7.2 13.3 %copy-start.27 = (s32[8]{0:T(128)S(1)}, s32[8]{0:T(128)}, u32[]{:S(2)}) copy-start(s32[8]{0:T(128)} %param.15) | copy-start | bytes 100
  7.2 13.5 %copy-start.21 = (s32[8]{0:T(128)S(1)}, s32[8]{0:T(128)}, u32[]{:S(2)}) copy-start(s32[8]{0:T(128)} %param.17) | copy-start | bytes 100
  7.2 14.1 %copy-start.29 = (f32[8]{0:T(128)S(1)}, f32[8]{0:T(128)}, u32[]{:S(2)}) copy-start(f32[8]{0:T(128)} %param.18) | copy-start | bytes 100
  7.2 14.2 %copy-start.26 = (f32[2,128]{1,0:T(2,128)S(1)}, f32[2,128]{1,0:T(2,128)}, u32[]{:S(2)}) copy-start(f32[2,128]{1,0:T(2,128)} %param.22) | copy-start | bytes 3076
  8.7 17.8 %copy-start.18 = (bf16[3,3,3,16,512]{4,3,2,1,0:T(8,128)(2,1)S(1)}, bf16[3,3,3,16,512]{4,3,2,1,0:T(8,128)(2,1)}, u32[]{:S(2)}) copy-start(bf16[3,3,3,16,512]{4,3,2,1,0:T(8,128)(2,1)} %param.14) | copy-start | bytes 1327108
  8.7 13.9 %collective-permute-start = (bf16[2,2,32,512]{3,2,1,0:T(8,128)(2,1)S(1)}, bf16[2,2,32,512]{3,2,1,0:T(8,128)(2,1)S(1)}, u32[]{:S(2)}, u32[]{:S(2)}) collective-permute-start(bf16[2,2,32,512]{3,2,1,0:T(8,128)(2,1)S(1)} %slice.274), channel_id=1, source_target_pairs={{0,8},{8,16},{16,24},{1,9},{9,17},{17,25},{2,10},{10,18},{18,26},{... | collective-permute-start | bytes 393224 | tf_op jit(solution)/shard_map/ppermute | solution.py:10
  15.5 29.0 %all-to-all-start = ((bf16[128,8,128]{0,2,1:T(8,128)(2,1)}), bf16[128,8,128]{0,2,1:T(8,128)(2,1)}, u32[]{:S(2)}, u32[]{:S(2)}) async-start(bf16[128,8,128]{0,2,1:T(8,128)(2,1)} %bitcast.89), calls=%async_computation | async-start | bytes 524288 | tf_op jit(solution)/shard_map/all_to_all | solution.py:171
  20.4 50.8 %reduce-scatter.7.cloned.1.call-start = ((), (), s32[]{:S(2)}) async-start(), calls=%async_computation.5 | async-start | bytes 327680
  22.7 4.0 %collective-permute-start.1 = (bf16[10,1,32,512]{3,2,1,0:T(8,128)(2,1)S(1)}, bf16[10,1,32,512]{3,2,1,0:T(8,128)(2,1)S(1)}, u32[]{:S(2)}, u32[]{:S(2)}) collective-permute-start(bf16[10,1,32,512]{3,2,1,0:T(8,128)(2,1)S(1)} %get-tuple-element.273), channel_id=1, source_target_pairs={{0,1},{1,2},{2,3},{3,4},{4,5},{5,6},{6,7},{8,9},{9,10},{10,11},{11... | collective-permute-start | bytes 983048 | tf_op jit(solution)/shard_map/ppermute | solution.py:20
  25.1 4.6 %collective-permute-start.2 = (bf16[10,1,32,512]{3,2,1,0:T(8,128)(2,1)S(1)}, bf16[10,1,32,512]{3,2,1,0:T(8,128)(2,1)S(1)}, u32[]{:S(2)}, u32[]{:S(2)}) collective-permute-start(bf16[10,1,32,512]{3,2,1,0:T(8,128)(2,1)S(1)} %get-tuple-element.274), channel_id=1, source_target_pairs={{1,0},{2,1},{3,2},{4,3},{5,4},{6,5},{7,6},{9,8},{10,9},{11,10},{12... | collective-permute-start | bytes 983048 | tf_op jit(solution)/shard_map/ppermute | solution.py:21
  40.0 3.7 %copy-start.19 = (bf16[1,128,64]{1,2,0:T(8,128)(2,1)S(1)}, bf16[1,128,64]{1,2,0:T(8,128)(2,1)}, u32[]{:S(2)}) copy-start(bf16[1,128,64]{1,2,0:T(8,128)(2,1)} %param.19) | copy-start | bytes 49156
  40.3 3.5 %copy-start.12 = (bf16[2048,3,1,128]{3,0,2,1:T(8,128)(2,1)S(1)}, bf16[2048,3,1,128]{3,0,2,1:T(8,128)(2,1)}, u32[]{:S(2)}) copy-start(bf16[2048,3,1,128]{3,0,2,1:T(8,128)(2,1)} %param.21) | copy-start | bytes 4718596
  42.6 119.0 %reduce-scatter.5.cloned.1.call-start = ((), (), s32[]{:S(2)}) async-start(), calls=%async_computation.4 | async-start | bytes 1966080 | tf_op jit(solution)/shard_map/reduce_scatter | solution.py:235
  43.5 28.5 %copy-start.22 = (f32[128]{0:T(128)}, f32[128]{0:T(128)S(1)}, u32[]{:S(2)}) copy-start(f32[128]{0:T(128)S(1)} %mul.598) | copy-start | bytes 1540
  43.7 28.3 %copy-start.24 = (f32[128]{0:T(128)}, f32[128]{0:T(128)S(1)}, u32[]{:S(2)}) copy-start(f32[128]{0:T(128)S(1)} %mul.661) | copy-start | bytes 1540
  87.9 1.9 %copy-start.2 = (bf16[1024,2048]{1,0:T(8,128)(2,1)}, bf16[1024,2048]{1,0:T(8,128)(2,1)S(1)}, u32[]{:S(2)}) copy-start(bf16[1024,2048]{1,0:T(8,128)(2,1)S(1)} %convolution_convert_fusion) | copy-start | bytes 12582916
  89.9 1.2 copy-start.3
  90.0 2.6 %copy-start.20 = (s32[512]{0:T(512)S(1)}, s32[512]{0:T(512)}, u32[]{:S(2)}) copy-start(s32[512]{0:T(512)} %broadcast_bitcast_fusion.3) | copy-start | bytes 6148
  92.6 2.3 %copy-start.5 = (bf16[1024,1,128]{2,0,1:T(8,128)(2,1)}, bf16[1024,1,128]{2,0,1:T(8,128)(2,1)S(1)}, u32[]{:S(2)}) copy-start(bf16[1024,1,128]{2,0,1:T(8,128)(2,1)S(1)} %get-tuple-element.409) | copy-start | bytes 786436 | tf_op jit(solution)/shard_map/while
  92.6 2.3 %copy-start.7 = (bf16[2,512,1,128]{3,1,2,0:T(8,128)(2,1)}, bf16[2,512,1,128]{3,1,2,0:T(8,128)(2,1)S(1)}, u32[]{:S(2)}) copy-start(bf16[2,512,1,128]{3,1,2,0:T(8,128)(2,1)S(1)} %get-tuple-element.407) | copy-start | bytes 786436 | tf_op jit(solution)/shard_map/while
  95.3 2.1 %copy-start.9 = (f32[2,512,1,128]{3,1,2,0:T(8,128)S(1)}, f32[2,512,1,128]{3,1,2,0:T(8,128)}, u32[]{:S(2)}) copy-start(f32[2,512,1,128]{3,1,2,0:T(8,128)} %get-tuple-element.392) | copy-start | bytes 1572868 | tf_op jit(solution)/shard_map/while
  95.4 4.3 %copy-start.16 = (f32[1024,1,128]{0,2,1:T(8,128)S(1)}, f32[1024,1,128]{0,2,1:T(8,128)}, u32[]{:S(2)}) copy-start(f32[1024,1,128]{0,2,1:T(8,128)} %get-tuple-element.390) | copy-start | bytes 1572868 | tf_op jit(solution)/shard_map/while
  98.9 0.8 copy-start.10
  99.7 2.2 %copy-start.13 = (bf16[2,512,1,128]{3,1,2,0:T(8,128)(2,1)S(1)}, bf16[2,512,1,128]{3,1,2,0:T(8,128)(2,1)}, u32[]{:S(2)}) copy-start(bf16[2,512,1,128]{3,1,2,0:T(8,128)(2,1)} %get-tuple-element.391) | copy-start | bytes 786436 | tf_op jit(solution)/shard_map/while
  101.1 0.8 copy-start.17
  101.9 2.3 %copy-start.6 = (bf16[1024,1,128]{2,0,1:T(8,128)(2,1)S(1)}, bf16[1024,1,128]{2,0,1:T(8,128)(2,1)}, u32[]{:S(2)}) copy-start(bf16[1024,1,128]{2,0,1:T(8,128)(2,1)} %copy-done.5) | copy-start | bytes 786436 | tf_op jit(solution)/shard_map/while
  101.9 2.3 %copy-start.8 = (bf16[2,512,1,128]{3,1,2,0:T(8,128)(2,1)S(1)}, bf16[2,512,1,128]{3,1,2,0:T(8,128)(2,1)}, u32[]{:S(2)}) copy-start(bf16[2,512,1,128]{3,1,2,0:T(8,128)(2,1)} %copy-done.7) | copy-start | bytes 786436 | tf_op jit(solution)/shard_map/while
  103.5 0.7 copy-start.14
  104.2 2.3 %copy-start.5 = (bf16[1024,1,128]{2,0,1:T(8,128)(2,1)}, bf16[1024,1,128]{2,0,1:T(8,128)(2,1)S(1)}, u32[]{:S(2)}) copy-start(bf16[1024,1,128]{2,0,1:T(8,128)(2,1)S(1)} %get-tuple-element.409) | copy-start | bytes 786436 | tf_op jit(solution)/shard_map/while
  104.2 2.3 %copy-start.7 = (bf16[2,512,1,128]{3,1,2,0:T(8,128)(2,1)}, bf16[2,512,1,128]{3,1,2,0:T(8,128)(2,1)S(1)}, u32[]{:S(2)}) copy-start(bf16[2,512,1,128]{3,1,2,0:T(8,128)(2,1)S(1)} %get-tuple-element.407) | copy-start | bytes 786436 | tf_op jit(solution)/shard_map/while
  106.9 2.3 %copy-start.9 = (f32[2,512,1,128]{3,1,2,0:T(8,128)S(1)}, f32[2,512,1,128]{3,1,2,0:T(8,128)}, u32[]{:S(2)}) copy-start(f32[2,512,1,128]{3,1,2,0:T(8,128)} %get-tuple-element.392) | copy-start | bytes 1572868 | tf_op jit(solution)/shard_map/while
  106.9 4.5 %copy-start.16 = (f32[1024,1,128]{0,2,1:T(8,128)S(1)}, f32[1024,1,128]{0,2,1:T(8,128)}, u32[]{:S(2)}) copy-start(f32[1024,1,128]{0,2,1:T(8,128)} %get-tuple-element.390) | copy-start | bytes 1572868 | tf_op jit(solution)/shard_map/while
  110.6 0.8 copy-start.10
  111.4 2.2 %copy-start.13 = (bf16[2,512,1,128]{3,1,2,0:T(8,128)(2,1)S(1)}, bf16[2,512,1,128]{3,1,2,0:T(8,128)(2,1)}, u32[]{:S(2)}) copy-start(bf16[2,512,1,128]{3,1,2,0:T(8,128)(2,1)} %get-tuple-element.391) | copy-start | bytes 786436 | tf_op jit(solution)/shard_map/while
  112.8 0.8 copy-start.17
  113.6 2.3 %copy-start.6 = (bf16[1024,1,128]{2,0,1:T(8,128)(2,1)S(1)}, bf16[1024,1,128]{2,0,1:T(8,128)(2,1)}, u32[]{:S(2)}) copy-start(bf16[1024,1,128]{2,0,1:T(8,128)(2,1)} %copy-done.5) | copy-start | bytes 786436 | tf_op jit(solution)/shard_map/while
  113.6 2.3 %copy-start.8 = (bf16[2,512,1,128]{3,1,2,0:T(8,128)(2,1)S(1)}, bf16[2,512,1,128]{3,1,2,0:T(8,128)(2,1)}, u32[]{:S(2)}) copy-start(bf16[2,512,1,128]{3,1,2,0:T(8,128)(2,1)} %copy-done.7) | copy-start | bytes 786436 | tf_op jit(solution)/shard_map/while
  115.2 0.7 copy-start.14
  115.9 2.6 %copy-start.1 = (f32[1024,1,128]{0,2,1:T(8,128)S(1)}, f32[1024,1,128]{0,2,1:T(8,128)}, u32[]{:S(2)}) copy-start(f32[1024,1,128]{0,2,1:T(8,128)} %get-tuple-element.71) | copy-start | bytes 1572868
  115.9 2.6 %copy-start.4 = (f32[1024,3,128]{0,2,1:T(8,128)S(1)}, f32[1024,3,128]{0,2,1:T(8,128)}, u32[]{:S(2)}) copy-start(f32[1024,3,128]{0,2,1:T(8,128)} %copy-done.3) | copy-start | bytes 4718596
  115.9 2.8 %copy-start.11 = (f32[2,512,1,128]{3,1,2,0:T(8,128)S(1)}, f32[2,512,1,128]{3,1,2,0:T(8,128)}, u32[]{:S(2)}) copy-start(f32[2,512,1,128]{3,1,2,0:T(8,128)} %get-tuple-element.70) | copy-start | bytes 1572868
  120.3 6.4 %copy-start.15 = (bf16[2,512,1,128]{3,1,2,0:T(8,128)(2,1)S(1)}, bf16[2,512,1,128]{3,1,2,0:T(8,128)(2,1)}, u32[]{:S(2)}) copy-start(bf16[2,512,1,128]{3,1,2,0:T(8,128)(2,1)} %get-tuple-element.69) | copy-start | bytes 786436
  126.1 6.7 %copy-start.23 = (f32[128]{0:T(128)S(1)}, f32[128]{0:T(128)}, u32[]{:S(2)}) copy-start(f32[128]{0:T(128)} %copy-done.22) | copy-start | bytes 1540
  126.1 6.7 %copy-start.25 = (f32[128]{0:T(128)S(1)}, f32[128]{0:T(128)}, u32[]{:S(2)}) copy-start(f32[128]{0:T(128)} %copy-done.24) | copy-start | bytes 1540
  128.2 32.0 %all-to-all-start.1 = ((bf16[8,2,8192]{2,1,0:T(2,128)(2,1)}), bf16[8,2,8192]{2,1,0:T(2,128)(2,1)S(1)}, u32[]{:S(2)}, u32[]{:S(2)}) async-start(bf16[8,2,8192]{2,1,0:T(2,128)(2,1)} %reshape.832), calls=%async_computation.1 | async-start | bytes 524288 | tf_op jit(solution)/shard_map/all_to_all | solution.py:222
Sparse Core Ops, SparseCore 0:
  42.7 28.4 reduce-scatter.6
  126.2 31.1 reduce-scatter.4
